TPU v7x, 256 devices: a whole 4x4x8 slice. The times are simulated.
256 devices in a mesh: kring: 16 (over y_lo, x, core), cuts: 16 (over z, y_hi).
Axes of the slice: x: 4, y: 4 (y_hi: 2, y_lo: 2; y = y_hi * 2 + y_lo), z: 8, core: 2. Of those that a mesh axis runs over, the one named last changes fastest.
Arguments:
- blocks: bfloat16 [16, 768, 4096], P('kring', None, 'cuts'), may hold values from -0.75 to 0.75
- vir_energy: bfloat16 [16, 768], P('kring'), may hold values from 0.29882812 to 3
- occ_energy: bfloat16 [16], P('kring'), may hold values from -1 to -0.19921875
- partner: int32 [1, 16], replicated, may hold values from 0 to 15, each once within a row
Outputs:
- gamma_own: bfloat16 [16, 768, 4096], P('kring', None, 'cuts')
- gamma_partner: bfloat16 [1, 16, 768, 4096], P(None, 'kring', None, 'cuts')
Inputs may be any that keep to these rules, and one draw needn't show every extreme that they name: Each row of partner names every k-point exactly once.
All inputs are finite; a program needn't handle non-finite values.
Results may differ from a plain program's by a relative error of at most 0.0055.
Values may be sent and summed in bfloat16 or wider, within the bound.
A program may use at most 64 MiB of HBM per device.

v0:
```python
import jax
import jax.numpy as jnp
from jax import lax
from jax.sharding import PartitionSpec as P


def on_device(blocks, vir_energy, occ_energy, partner):
    local_count = blocks.shape[0]
    first_kpoint = lax.axis_index("kring") * local_count
    wanted = lax.dynamic_slice_in_dim(partner, first_kpoint, local_count, 1)
    visitor = (
        lax.all_gather(blocks, "kring", axis=0, tiled=True),
        lax.all_gather(vir_energy, "kring", axis=0, tiled=True),
        lax.all_gather(occ_energy, "kring", axis=0, tiled=True),
    )
    row_ids = jnp.arange(visitor[0].shape[0], dtype=jnp.int32)
    onehot = (wanted[:, :, None] == row_ids[None, None, :]).astype(jnp.bfloat16)
    got_blocks = jnp.einsum(
        "qkn,nvp->qkvp", onehot, visitor[0], preferred_element_type=jnp.bfloat16
    )
    got_vir = jnp.einsum("qkn,nv->qkv", onehot, visitor[1], preferred_element_type=jnp.bfloat16)
    got_occ = jnp.einsum("qkn,n->qk", onehot, visitor[2], preferred_element_type=jnp.bfloat16)
    partner_grid = [[None] * local_count]
    own_block = blocks[0]
    own_vir = vir_energy[0].astype(jnp.float32)
    own_occ = occ_energy[0].astype(jnp.float32)
    partner_blocks = [got_blocks[0, 0]]
    denominators = [
        own_vir[:, None]
        + got_vir[0, 0].astype(jnp.float32)[None, :]
        - (own_occ + got_occ[0, 0].astype(jnp.float32))
    ]
    columns = []
    for partner_block, denominator in zip(partner_blocks, denominators):
        integral = lax.dot_general(
            own_block, partner_block, (((1,), (1,)), ((), ())), preferred_element_type=jnp.float32
        )
        columns.append(integral / denominator)
    summed_rows = lax.psum_scatter(columns[0], "cuts", scatter_dimension=0, tiled=True)
    gathered = lax.all_gather(summed_rows.astype(jnp.bfloat16), "cuts", axis=0, tiled=True)
    paired = (2.0 * gathered.astype(jnp.float32) - gathered.T.astype(jnp.float32)).astype(
        jnp.bfloat16
    )
    own_acc = jnp.dot(paired, partner_blocks[0], preferred_element_type=jnp.float32)
    back_term = lax.dot_general(
        paired, own_block, (((0,), (0,)), ((), ())), preferred_element_type=jnp.float32
    )
    partner_grid[0][0] = back_term.astype(jnp.bfloat16)
    own_list = [own_acc.astype(jnp.bfloat16)]
    gamma_own = jnp.stack(own_list)
    gamma_partner = jnp.stack([jnp.stack(grid_row) for grid_row in partner_grid])
    return (gamma_own, gamma_partner)


def solution(mesh):
    return jax.shard_map(
        on_device,
        mesh=mesh,
        in_specs=(P("kring", None, "cuts"), P("kring", None), P("kring"), P()),
        out_specs=(P("kring", None, "cuts"), P(None, "kring", None, "cuts")),
        check_vma=False,
    )
```

profile of v0, /device:TPU:2, one launch (start us, length us, event | category | flops | bytes accessed | tf_op | source)
XLA Modules:
  0.0 378.2 jit_solution(11107149817863094085)
XLA Ops:
  7.2 0.0 copy-start
  7.2 0.0 all-gather.4.cloned.1.call-start
  7.2 0.7 all-gather.4.cloned.1.call-update
  7.9 0.0 reduce-scatter.4.cloned.1.call-start
  8.6 1.3 dynamic-slice
  9.9 0.8 dynamic-update-slice
  10.6 26.8 %all-reduce = bf16[16]{0:T(256)(128)(2,1)S(1)} all-reduce(bf16[16]{0:T(256)(128)(2,1)S(1)} %dynamic-update-slice), channel_id=1, replica_groups=mesh['kring'=16,'cuts'=16] {'kring'}, use_global_device_ids=true, to_apply=%add | all-reduce | flops 16 | bytes 64
  37.5 0.0 copy-done
  37.5 0.6 constant_dynamic-slice_fusion
  38.0 21.1 %all-gather = bf16[16,1,768]{2,1,0:T(2,128)(2,1)S(1)} all-gather(bf16[1,1,768]{2,1,0:T(2,128)(2,1)} %bitcast.38), channel_id=1, replica_groups=mesh['kring'=16,'cuts'=16] {'kring'}, dimensions={0}, use_global_device_ids=true | all-gather | bytes 26112 | tf_op jit(solution)/shard_map/all_gather | solution.py:13
  59.2 0.8 convolution_reduce_fusion
  59.9 1.3 select_reduce_fusion
  61.8 0.7 convert_reduce_fusion
  62.5 0.0 copy-start.4
  62.5 0.0 all-gather.4.cloned.1.call-done
  62.5 7.2 %fusion = bf16[1,768,256]{2,0,1:T(2,128)(2,1)S(1)} fusion(bf16[16,768,256]{2,1,0:T(8,128)(2,1)} %all-gather.4.cloned.1.call-done, s32[]{:T(128)} %bitcast), kind=kOutput, calls=%fused_computation | convolution fusion | flops 6291472 | bytes 6684676 | tf_op jit(solution)/shard_map/qkn,nvp->qkvp/dot_general | solution.py:18
  69.7 0.0 copy-start.2
  69.7 0.9 copy-done.2
  70.6 0.0 copy-done.4
  70.6 0.5 bitcast_divide_fusion
  71.1 2.0 copy.16
  73.1 0.0 reduce-scatter.4.cloned.1.call-update
  73.1 0.0 all-gather.6.cloned.1.call-start
  73.2 212.3 %reduce-scatter.4.cloned.1.call-done = f32[48,768]{1,0:T(8,128)} async-done(((f32[768,768]{1,0:T(8,128)}), f32[48,768]{1,0:T(8,128)}) %reduce-scatter.4.cloned.1.call-update) | async-done | bytes 147472 | tf_op jit(solution)/shard_map/reduce_scatter | solution.py:39
  285.5 1.6 convert_element_type.52
  287.1 0.0 all-gather.6.cloned.1.call-update
  287.1 79.2 %all-gather.6.cloned.1.call-done = bf16[768,768]{1,0:T(8,128)(2,1)} async-done(((bf16[48,768]{1,0:T(8,128)(2,1)}), bf16[768,768]{1,0:T(8,128)(2,1)}) %all-gather.6.cloned.1.call-update) | async-done | bytes 1179664 | tf_op jit(solution)/shard_map/all_gather | solution.py:40
  366.3 0.0 copy-start.1
  366.3 1.7 copy.11
  368.0 0.0 copy-done.1
  368.0 0.0 copy-start.3
  368.0 2.3 fusion.4
  370.3 0.0 copy-done.3
  370.3 1.3 fusion.3
  (2 shorter events, 0.0 us)
Async XLA Ops:
  7.2 30.3 %copy-start = (s32[1,16]{1,0:T(1,128)S(1)}, s32[1,16]{1,0:T(1,128)}, u32[]{:S(2)}) copy-start(s32[1,16]{1,0:T(1,128)} %param.7) | copy-start | bytes 196
  7.2 55.3 %all-gather.4.cloned.1.call-start = ((), (), s32[]{:S(2)}) async-start(), calls=%async_computation.1 | async-start | bytes 6684672 | tf_op jit(solution)/shard_map/all_gather | solution.py:12
  7.9 277.6 %reduce-scatter.4.cloned.1.call-start = ((), (), s32[]{:S(2)}) async-start(), calls=%async_computation.3 | async-start | bytes 2506752 | tf_op jit(solution)/shard_map/reduce_scatter | solution.py:39
  62.5 8.1 %copy-start.4 = (bf16[1,768,256]{2,1,0:T(8,128)(2,1)S(1)}, bf16[1,768,256]{2,1,0:T(8,128)(2,1)}, u32[]{:S(2)}) copy-start(bf16[1,768,256]{2,1,0:T(8,128)(2,1)} %param.4) | copy-start | bytes 1179652
  69.7 0.9 copy-start.2
  73.1 293.2 %all-gather.6.cloned.1.call-start = ((), (), s32[]{:S(2)}) async-start(), calls=%async_computation.2 | async-start | bytes 1253376 | tf_op jit(solution)/shard_map/all_gather | solution.py:40
  366.3 1.7 copy-start.1
  368.0 2.3 copy-start.3
Sparse Core Ops, SparseCore 0:
  9.9 47.9 all-gather.3
  73.3 212.1 reduce-scatter.3
  288.7 77.6 all-gather.5
where the time goes:
time: 378 us
  waiting for transfers between devices  292 us (77%)
  blocking collectives  47.9 us (13%)
  between operations  15.1 us (4%)
  matrix products  12.1 us (3%)
  local copies, waits for them, and re-layouts  7.17 us (2%)
    reduce_scatter x1, waiting for transfers between devices, on_device(): lax.psum_scatter(columns[0], 'cuts', scatter_dimension=0, tiled=True)  212 us
    all_gather x1, waiting for transfers between devices, on_device(): lax.all_gather(summed_rows.astype(jnp.bfloat16), 'cuts', axis=0, tiled=True)  79.2 us
    unnamed x1, blocking collectives  26.8 us
    all_gather x1, blocking collectives, on_device(): lax.all_gather(vir_energy, 'kring', axis=0, tiled=True)  21.1 us
  transfers between devices with their start and end apart: 3, of which 2 were waited for; matrix products, arithmetic and copies ran while one was open for 1% of the time, Pallas kernels for 0%

commit v1 on v0

v1 whole, which is shorter than its diff:
```python
import functools

import jax
import jax.numpy as jnp
from jax import lax
from jax.experimental import pallas as pl
from jax.experimental.pallas import tpu as pltpu
from jax.sharding import PartitionSpec as P

MESH = pl.DeviceIdType.MESH
DMA = pltpu.SemaphoreType.DMA
BF = jnp.bfloat16
F32 = jnp.float32

NK = 16
VIRT = 768
COLS = 256
ROWS = 48
HALF = 384
COL_A = pl.ds(0, HALF)
COL_B = pl.ds(HALF, HALF)
N_MSG = 100


def nt_dot(left, right):
    return lax.dot_general(left, right, (((1,), (1,)), ((), ())), preferred_element_type=F32)


def kernel(
    part, own, energy, out_own, out_mate,
    mid, stage, mate, all_energy, own_vir, integral,
    a_send, a_recv, a_direct, a_relay, a_final, a_ysend, a_yrecv,
    b_send, b_recv, b_direct, b_relay, b_final, b_ysend, b_yrecv,
    direct, send_sems, recv_sems,
):
    k = lax.axis_index("kring")
    c = lax.axis_index("cuts")
    z = c // 2
    h = lax.rem(c, 2)
    g = 1 - h

    def zpos(step):
        return lax.rem(z + step + 8, 8)

    def zdev(step):
        return (k, zpos(step) * 2 + h)

    ydev = (k, z * 2 + g)
    ring = [lax.rem(k + i, NK) for i in range(1, NK)]

    copies = []

    def send(src, dst, dev):
        copy = pltpu.make_async_remote_copy(
            src_ref=src,
            dst_ref=dst,
            send_sem=send_sems.at[len(copies)],
            recv_sem=recv_sems.at[len(copies)],
            device_id=dev,
            device_id_type=MESH,
        )
        copy.start()
        copies.append(copy)
        return copy

    barrier = pltpu.get_barrier_semaphore()
    peers = [(j, c) for j in ring] + [zdev(s) for s in (1, -1, 2, -2)] + [ydev]
    for dev in peers:
        pl.semaphore_signal(barrier, inc=1, device_id=dev, device_id_type=MESH)
    pl.semaphore_wait(barrier, len(peers))

    def piece(j):
        return pl.ds(pl.multiple_of(j * ROWS, ROWS), ROWS)

    first = [send(own.at[piece(j)], mid.at[k], (j, c)) for j in ring]
    mid[pl.ds(k, 1)] = own[piece(k)][None]
    all_energy[pl.ds(k, 1)] = energy[...][None]
    own_row = jnp.concatenate([energy[i : i + 1] for i in range(6)], axis=1)
    own_vir[...] = jnp.broadcast_to(own_row, (128, VIRT)).T
    for copy in first:
        copy.wait_recv()
    second = []
    for j in ring:
        stage[pl.ds(j, 1)] = mid[pl.ds(part[j], 1)]
        second.append(send(stage.at[j], mate.at[piece(k)], (j, c)))
    mate[piece(k)] = mid[part[k]]
    third = [send(energy, all_energy.at[k], (j, c)) for j in ring]
    for copy in second:
        copy.wait_recv()

    other = pl.ds(pl.multiple_of(g * HALF, HALF), HALF)
    mine = pl.ds(pl.multiple_of(h * HALF, HALF), HALF)
    b_ysend[...] = nt_dot(own[other], mate[COL_B]).astype(BF).reshape(8, ROWS, HALF)
    b_y = send(b_ysend, b_yrecv, ydev)
    for r in range(2):
        integral[r, :, :, COL_A] = nt_dot(own[pl.ds(r * HALF, HALF)], mate[COL_A]).reshape(8, ROWS, HALF)

    def reduce_start(chunk, out_buf, recv_buf, direct_buf, sign):
        plan = ((-3, -1, recv_buf.at[0]), (-4, -2, recv_buf.at[1]), (3, 1, recv_buf.at[2]),
                (-1, -1, direct_buf.at[0]), (1, 1, direct_buf.at[1]))
        sent = []
        for i, (dest, hop, target) in enumerate(plan):
            out_buf[i] = chunk(zpos(sign * dest)).astype(BF)
            sent.append(send(out_buf.at[i], target, zdev(sign * hop)))
        return sent

    def reduce_relay(chunk, sent, recv_buf, relay_buf, final_buf, sign):
        sent[0].wait_recv()
        sent[1].wait_recv()
        relay_buf[0] = (chunk(zpos(-2 * sign)) + recv_buf[0].astype(F32) + recv_buf[1].astype(F32)).astype(BF)
        near = send(relay_buf.at[0], final_buf.at[0], zdev(-2 * sign))
        sent[2].wait_recv()
        relay_buf[1] = (chunk(zpos(2 * sign)) + recv_buf[2].astype(F32)).astype(BF)
        far = send(relay_buf.at[1], final_buf.at[1], zdev(2 * sign))
        return [near, far]

    def reduce_end(chunk, sent, relayed, direct_buf, final_buf):
        for copy in sent[3:] + relayed:
            copy.wait_recv()
        return (chunk(z) + (direct_buf[0].astype(F32) + direct_buf[1].astype(F32))) + (
            final_buf[0].astype(F32) + final_buf[1].astype(F32)
        )

    def chunk_a(t):
        return integral[:, t, :, COL_A]

    def chunk_b(t):
        return integral[h, t, :, COL_B]

    a_sent = reduce_start(chunk_a, a_send, a_recv, a_direct, 1)
    integral[h, :, :, COL_B] = nt_dot(own[mine], mate[COL_B]).reshape(8, ROWS, HALF)
    b_y.wait_recv()
    integral[h, :, :, COL_B] += b_yrecv[...].astype(F32)
    b_sent = reduce_start(chunk_b, b_send, b_recv, b_direct, -1)
    a_relayed = reduce_relay(chunk_a, a_sent, a_recv, a_relay, a_final, 1)
    b_relayed = reduce_relay(chunk_b, b_sent, b_recv, b_relay, b_final, -1)

    for copy in third:
        copy.wait_recv()
    mate_energy = all_energy[part[k]]
    mate_row = jnp.concatenate([mate_energy[i : i + 1] for i in range(6)], axis=1)
    occupied = energy[6:7, 0:1] + mate_energy[6:7, 0:1]
    slot = h * 8 + z
    own_column = own_vir[piece(slot), 0:1]

    def amplitudes(total, cols):
        return (total / ((own_column + mate_row[:, cols]) - occupied)).astype(BF)

    total = reduce_end(chunk_a, a_sent, a_relayed, a_direct, a_final)
    integral[:, z, :, COL_A] = total
    a_ysend[...] = integral[g, z, :, COL_A].astype(BF)
    a_y = send(a_ysend, a_yrecv, ydev)

    def spread(at, cols, dev):
        view = direct.at[at, :, cols]
        return send(view, view, dev)

    def gather_start(at, cols):
        return [spread(at(0), cols, zdev(s)) for s in (1, -1, 2, -2)]

    def gather_relay(at, cols, sent, sign):
        sent[2 if sign > 0 else 3].wait_recv()
        on = [spread(at(-2 * sign), cols, zdev(sign * s)) for s in (2, 1)]
        sent[3 if sign > 0 else 2].wait_recv()
        back = [spread(at(2 * sign), cols, zdev(-sign))]
        return on + back

    def at_mine(step):
        return h * 8 + zpos(step)

    def at_other(step):
        return g * 8 + zpos(step)

    total = reduce_end(chunk_b, b_sent, b_relayed, b_direct, b_final)
    direct[slot, :, COL_B] = amplitudes(total, slice(HALF, VIRT))
    b_out = gather_start(at_mine, COL_B)
    b_cross = [spread(slot, COL_B, ydev)]

    a_y.wait_recv()
    total = integral[h, z, :, COL_A] + a_yrecv[...].astype(F32)
    direct[slot, :, COL_A] = amplitudes(total, slice(0, HALF))
    a_cross = spread(slot, COL_A, ydev)
    a_out = gather_start(at_mine, COL_A)

    b_on = gather_relay(at_mine, COL_B, b_out, -1)
    b_cross += [spread(at_mine(s), COL_B, ydev) for s in (2, -2)]
    for copy, s in ((b_out[0], -1), (b_out[1], 1)):
        copy.wait_recv()
        b_cross.append(spread(at_mine(s), COL_B, ydev))
    a_cross.wait_recv()
    a_other = gather_start(at_other, COL_A)
    a_on = gather_relay(at_mine, COL_A, a_out, 1)
    for copy, s in ((b_on[2], -3), (b_on[1], 3), (b_on[0], 4)):
        copy.wait_recv()
        b_cross.append(spread(at_mine(s), COL_B, ydev))
    a_other_on = gather_relay(at_other, COL_A, a_other, 1)
    for copy in a_out[:2] + a_on + a_other[:2] + a_other_on + b_cross:
        copy.wait_recv()

    amp = direct[...].reshape(VIRT, VIRT).astype(F32)
    flip = amp.T
    paired = (2.0 * amp - flip).astype(BF)
    out_own[...] = jnp.dot(paired, mate[...], preferred_element_type=F32).astype(BF)
    turned = (2.0 * flip - amp).astype(BF)
    out_mate[...] = jnp.dot(turned, own[...], preferred_element_type=F32).astype(BF)
    for copy in copies:
        copy.wait_send()


def on_device(blocks, vir_energy, occ_energy, partner):
    vir = vir_energy.astype(F32).reshape(6, 128)
    occ = jnp.broadcast_to(occ_energy.astype(F32).reshape(1, 1), (2, 128))
    energy = jnp.concatenate([vir, occ], axis=0)
    vmem = pl.BlockSpec(memory_space=pltpu.VMEM)
    chunk = (2, ROWS, HALF)
    half = (ROWS, HALF)
    gamma_own, gamma_mate = pl.pallas_call(
        kernel,
        out_shape=[jax.ShapeDtypeStruct((VIRT, COLS), BF)] * 2,
        in_specs=[pl.BlockSpec(memory_space=pltpu.SMEM), vmem, vmem],
        out_specs=[vmem, vmem],
        scratch_shapes=[
            pltpu.VMEM((NK, ROWS, COLS), BF),
            pltpu.VMEM((NK, ROWS, COLS), BF),
            pltpu.VMEM((VIRT, COLS), BF),
            pltpu.VMEM((NK, 8, 128), F32),
            pltpu.VMEM((VIRT, 128), F32),
            pltpu.VMEM((2, 8, ROWS, VIRT), F32),
            pltpu.VMEM((5,) + chunk, BF),
            pltpu.VMEM((3,) + chunk, BF),
            pltpu.VMEM((2,) + chunk, BF),
            pltpu.VMEM((2,) + chunk, BF),
            pltpu.VMEM((2,) + chunk, BF),
            pltpu.VMEM(half, BF),
            pltpu.VMEM(half, BF),
            pltpu.VMEM((5,) + half, BF),
            pltpu.VMEM((3,) + half, BF),
            pltpu.VMEM((2,) + half, BF),
            pltpu.VMEM((2,) + half, BF),
            pltpu.VMEM((2,) + half, BF),
            pltpu.VMEM((8,) + half, BF),
            pltpu.VMEM((8,) + half, BF),
            pltpu.VMEM((NK, ROWS, VIRT), BF),
            DMA((N_MSG,)),
            DMA((N_MSG,)),
        ],
        compiler_params=pltpu.CompilerParams(
            collective_id=0, has_side_effects=True, vmem_limit_bytes=56 * 1024 * 1024
        ),
        name="pair_window",
    )(partner.reshape(NK), blocks[0], energy)
    return gamma_own[None], gamma_mate[None, None]


def solution(mesh):
    return jax.shard_map(
        on_device,
        mesh=mesh,
        in_specs=(P("kring", None, "cuts"), P("kring", None), P("kring"), P()),
        out_specs=(P("kring", None, "cuts"), P(None, "kring", None, "cuts")),
        check_vma=False,
    )
```

time: 378 us -> 69.1 us (0.18)
  waiting for transfers between devices: 292 us -> 0 us
  Pallas kernels: 0 us -> 62.9 us
  blocking collectives: 47.9 us -> 0 us
  between operations: 15.1 us -> 1.31 us
  matrix products: 12.1 us -> 0 us
  local copies, waits for them, and re-layouts: 7.17 us -> 3.24 us
    reduce_scatter x1 -> x0, waiting for transfers between devices: 212 us -> none  [on_device(): lax.psum_scatter(columns[0], 'cuts', scatter_dimension=0, tiled=True)]
    all_gather x2 -> x0, waiting for transfers between devices: 79.3 us -> none  [the longest x1 79.2 us: on_device(): lax.all_gather(summed_rows.astype(jnp.bfloat16), 'cuts', axis=0, tiled=True)]
    pallas_call x0 -> x1, Pallas kernels: none -> 62.9 us  [on_device(): pl.pallas_call(kernel, out_shape=[jax.ShapeDtypeStruct((VIRT, COLS), BF)]...]
    unnamed x1 -> x0, blocking collectives: 26.8 us -> none
    all_gather x1 -> x0, blocking collectives: 21.1 us -> none  [on_device(): lax.all_gather(vir_energy, 'kring', axis=0, tiled=True)]
    dot_general x5 -> x0, matrix products: 12.1 us -> none  [the longest x1 7.18 us: on_device(): jnp.einsum('qkn,nvp->qkvp', onehot, visitor[0], preferred_element_type=jn...]
  transfers between devices with their start and end apart: 3 -> 0, of which waited for: 2 -> 0; matrix products, arithmetic and copies ran while one was open for 1% -> 0% of each run, Pallas kernels for 0% -> 0%
where the time goes in v1:
time: 69.1 us; the launch traced here: 68.1 us
  Pallas kernels  62.9 us (91%)
  local copies, waits for them, and re-layouts  3.24 us (5%)
  between operations  1.31 us (2%)
    pallas_call x1, Pallas kernels, on_device(): pl.pallas_call(kernel, out_shape=[jax.ShapeDtypeStruct((VIRT, COLS), BF)]...  62.9 us
    unnamed x6, local copies, waits for them, and re-layouts  3.24 us

profile of v1, /device:TPU:2, one launch (start us, length us, event | category | flops | bytes accessed | tf_op | source)
XLA Modules:
  0.0 68.1 jit_solution(2844084963904740913)
XLA Ops:
  1.3 0.0 copy-start.1
  1.3 0.7 copy-done.1
  2.0 0.6 pad_convert_fusion.energy
  2.6 62.9 %pair_window.1 = (bf16[768,256]{1,0:T(8,128)(2,1)}, bf16[768,256]{1,0:T(8,128)(2,1)}) custom-call(s32[16]{0:T(128)} %bitcast.11, bf16[768,256]{1,0:T(8,128)(2,1)} %bitcast.7, f32[8,128]{1,0:T(8,128)} %pad_convert_fusion.energy), custom_call_target="tpu_custom_call" | custom-call | tf_op jit(solution)/shard_map/pair_window/pallas_call | solution.py:217
  65.5 0.0 copy-start
  65.6 1.8 %copy.9 = bf16[1,768,256]{2,1,0:T(8,128)(2,1)} copy(bf16[1,768,256]{2,1,0:T(8,128)(2,1)} %bitcast.9) | data formatting | bytes 786432
  67.4 0.0 copy-done
  67.4 0.7 %copy.10 = bf16[1,1,768,256]{3,2,1,0:T(8,128)(2,1)} copy(bf16[1,1,768,256]{3,2,1,0:T(8,128)(2,1)S(1)} %bitcast.8) | data formatting | bytes 786432
  (1 shorter events, 0.0 us)
Async XLA Ops:
  1.3 0.7 %copy-start.1 = (bf16[1,768]{1,0:T(2,128)(2,1)S(1)}, bf16[1,768]{1,0:T(2,128)(2,1)}, u32[]{:S(2)}) copy-start(bf16[1,768]{1,0:T(2,128)(2,1)} %param.5) | copy-start | bytes 4612
  65.5 1.8 %copy-start = (bf16[768,256]{1,0:T(8,128)(2,1)S(1)}, bf16[768,256]{1,0:T(8,128)(2,1)}, u32[]{:S(2)}) copy-start(bf16[768,256]{1,0:T(8,128)(2,1)} %get-tuple-element.5) | copy-start | bytes 1179652

commit v2 on v0

v2 whole, which is shorter than its diff:
```python
import jax
import jax.numpy as jnp
from jax import lax
from jax.experimental import pallas as pl
from jax.experimental.pallas import tpu as pltpu
from jax.sharding import PartitionSpec as P

MESH = pl.DeviceIdType.MESH
DMA = pltpu.SemaphoreType.DMA
BF = jnp.bfloat16
F32 = jnp.float32

NK = 16
VIRT = 768
COLS = 256
ROWS = 48
BAND = 96
HALF = 384
FAR_FIRST = (6, 2, 5, 3, 7, 1, 4, 0)
N_MSG = 100


def nt_dot(left, right):
    return lax.dot_general(left, right, (((1,), (1,)), ((), ())), preferred_element_type=F32)


def rows_at(index, size):
    return pl.ds(pl.multiple_of(index * size, size), size)


def kernel(
    part, own, energy, out_own, out_mate,
    mid, stage, own_pair, mate_pair, mate, all_energy, mate_energy, own_vir, denominator,
    integral, r_send, r_recv, r_direct, r_relay, r_final, away, amp,
    send_sems, recv_sems, mate_sems,
):
    k = lax.axis_index("kring")
    c = lax.axis_index("cuts")
    z = c // 2
    h = lax.rem(c, 2)
    g = 1 - h
    pair = k // 2
    q = lax.rem(k, 2)
    r = 1 - q
    work = 2 * pair + h
    sign = 1 - 2 * q

    def zpos(step):
        return lax.rem(z + step + 8, 8)

    def device(core, step, plane):
        return (2 * pair + core, 2 * zpos(step) + plane)

    other_core = (2 * pair + r, c)
    ids = {}

    def describe(name, src, dst, dev):
        at = ids.setdefault(name, len(ids))
        return pltpu.make_async_remote_copy(
            src_ref=src, dst_ref=dst, send_sem=send_sems.at[at], recv_sem=recv_sems.at[at],
            device_id=dev, device_id_type=MESH,
        )

    def send(name, src, dst, dev):
        copy = describe(name, src, dst, dev)
        copy.start()
        return copy

    def arrived(name, ref):
        describe(name, ref, ref, other_core).wait_recv()

    def left(name, ref):
        describe(name, ref, ref, other_core).wait_send()

    barrier = pltpu.get_barrier_semaphore()
    kring = [(2 * lax.rem(pair + i, 8) + core, i, core) for i in FAR_FIRST for core in (q, r)][:-2] + [
        (2 * pair + r, 0, r)
    ]
    peers = [(j, c) for j, _, _ in kring]
    peers += [(2 * lax.rem(pair + i, 8) + q, 2 * z + g) for i in range(8)] + [device(r, 0, g)]
    peers += [device(core, s, h) for core in (q, r) for s in (1, -1, 2, -2)]
    for dev in peers:
        pl.semaphore_signal(barrier, inc=1, device_id=dev, device_id_type=MESH)
    pl.semaphore_wait(barrier, len(peers))

    sent = []
    for n, (j, _, core) in enumerate(kring):
        sent.append(send(f"spread{n}", own.at[rows_at(core * 8 + j // 2, ROWS)], mid.at[k], (j, c)))

    mine_half = rows_at(q, HALF)

    @pl.when(q == h)
    def _():
        send("own_core", own, own_pair.at[h], other_core)

    @pl.when(q != h)
    def _():
        for core in (0, 1):
            half = pl.ds(core * HALF, HALF)
            send(f"own_y{core}", own.at[half], own_pair.at[h, half], device(core, 0, g))

    @pl.when(q == h)
    def _():
        own_pair[pl.ds(h, 1)] = own[...][None]

    mid[pl.ds(k, 1)] = own[rows_at(q * 8 + pair, ROWS)][None]
    all_energy[pl.ds(k, 1)] = energy[...][None]
    for n in range(15):
        arrived(f"spread{n}", mid.at[0])
    n = 0
    for i in FAR_FIRST:
        for plane in (g, h):
            target = lax.rem(pair + i, 8)
            wanted = mid[pl.ds(part[2 * target + plane], 1)]
            if i == 0 and plane is h:
                mate_pair[pl.ds(h, 1), rows_at(pair, ROWS)] = wanted
                continue
            stage[n] = wanted[0]
            sent.append(
                send(f"pick{n}", stage.at[n], mate_pair.at[h, rows_at(pair, ROWS)], (2 * target + q, 2 * z + plane))
            )
            n += 1

    def own_y_arrived():
        ref = own_pair.at[g, mine_half]
        at0 = ids["own_y0"]
        pltpu.make_async_remote_copy(
            src_ref=ref, dst_ref=ref, send_sem=send_sems.at[at0], recv_sem=recv_sems.at[at0 + q],
            device_id=other_core, device_id_type=MESH,
        ).wait_recv()

    own_y_arrived()
    sent.append(send("own_swap", own_pair.at[g, mine_half], own_pair.at[g, mine_half], other_core))
    for n, (j, _, _) in enumerate(kring):
        sent.append(send(f"energy{n}", energy, all_energy.at[k], (j, c)))

    @pl.when(q != h)
    def _():
        arrived("own_core", own)

    for n in range(15):
        arrived(f"pick{n}", stage.at[0])
    arrived("own_swap", own_pair.at[g, mine_half])

    for b in range(4):
        band = pl.ds(b * 192, 192)
        integral[pl.ds(2 * b, 2)] = (
            nt_dot(own_pair[0, band], mate_pair[0]) + nt_dot(own_pair[1, band], mate_pair[1])
        ).reshape(2, BAND, HALF)

    plan = ((-4, -2, r_recv.at[1]), (-3, -1, r_recv.at[0]), (3, 1, r_recv.at[2]),
            (-1, -1, r_direct.at[0]), (1, 1, r_direct.at[1]))
    starts = []
    for i, (dest, hop, target) in enumerate(plan):
        r_send[i] = integral[zpos(sign * dest)].astype(BF)
        starts.append(send(f"part{i}", r_send.at[i], target, device(q, sign * hop, h)))
    sent += starts

    def mate_copy(dst_core, plane, src):
        return pltpu.make_async_remote_copy(
            src_ref=src, dst_ref=mate.at[mine_half], send_sem=mate_sems.at[2], recv_sem=mate_sems.at[q],
            device_id=device(dst_core, 0, plane), device_id_type=MESH,
        )

    mate_copy(h, g, mate_pair.at[g]).start()

    @pl.when(q == h)
    def _():
        mate[mine_half] = mate_pair[h]

    @pl.when(q != h)
    def _():
        send("mate_core", mate_pair.at[h], mate.at[mine_half], other_core)

    for n in range(15):
        arrived(f"energy{n}", energy)
    mate_energy[...] = all_energy[part[work]]
    work_energy = all_energy[work]
    own_row = jnp.concatenate([work_energy[i : i + 1] for i in range(6)], axis=1)
    own_vir[...] = jnp.broadcast_to(own_row, (128, VIRT)).T
    mate_row = jnp.concatenate([mate_energy[pl.ds(q * 3 + i, 1)] for i in range(3)], axis=1)
    occupied = work_energy[6:7, 0:1] + mate_energy[6:7, 0:1]
    denominator[...] = (own_vir[rows_at(z, BAND), 0:1] + mate_row) - occupied

    starts[0].wait_recv()
    starts[1].wait_recv()
    r_relay[0] = (integral[zpos(-2 * sign)] + r_recv[0].astype(F32) + r_recv[1].astype(F32)).astype(BF)
    sent.append(send("relay0", r_relay.at[0], r_final.at[0], device(q, -2 * sign, h)))
    starts[2].wait_recv()
    r_relay[1] = (integral[zpos(2 * sign)] + r_recv[2].astype(F32)).astype(BF)
    sent.append(send("relay1", r_relay.at[1], r_final.at[1], device(q, 2 * sign, h)))
    starts[3].wait_recv()
    starts[4].wait_recv()
    total = integral[z] + (r_direct[0].astype(F32) + r_direct[1].astype(F32))
    for n in range(2):
        arrived(f"relay{n}", r_final.at[0])
    total = total + (r_final[0].astype(F32) + r_final[1].astype(F32))
    chunk = (total / denominator[...]).astype(BF)

    block = amp.at[0, 0]
    near = (2, -2, 1, -1)

    def pass_on(tag, half, way):
        arrived(f"{tag}first{2 * way}", block)
        out = [
            send(f"{tag}on{s}", amp.at[half, zpos(-2 * way)], amp.at[half, zpos(-2 * way)], device(q, s * way, h))
            for s in (2, 1)
        ]
        arrived(f"{tag}first{-2 * way}", block)
        view = amp.at[half, zpos(2 * way)]
        out.append(send(f"{tag}back", view, view, device(q, -way, h)))
        return out

    def late(tag, way):
        return ((f"{tag}on2", -4 * way), (f"{tag}on1", -3 * way), (f"{tag}back", 3 * way))

    @pl.when(q == h)
    def _():
        amp[q, z] = chunk
        view = amp.at[q, z]
        out = [send(f"b_first{s}", view, view, device(q, s, h)) for s in near]

        def cross(step):
            view = amp.at[q, zpos(step)]
            out.append(send(f"cross{step}", view, view, device(q, 0, g)))

        cross(0)
        out.extend(pass_on("b_", q, 1))
        cross(-2)
        cross(2)
        out.extend(pass_on("a_", r, -1))
        for s in (1, -1):
            arrived(f"b_first{s}", block)
            cross(-s)
        for name, step in late("b_", 1):
            arrived(name, block)
            cross(step if step > -4 else 4)
        arrived("a_own", block)
        for s in (1, -1):
            arrived(f"a_first{s}", block)
        for name, _ in late("a_", -1):
            arrived(name, block)
        arrived("mate_core", mate.at[mine_half])
        for copy in out:
            copy.wait_send()

    @pl.when(q != h)
    def _():
        away[...] = chunk
        target = amp.at[q, z]
        out = [send("a_y", away, target, device(r, 0, g))]
        out += [send(f"a_first{s}", away, target, device(r, s, h)) for s in near]
        out += [send("a_own", away, target, other_core)]
        arrived("a_y", block)
        view = amp.at[r, z]
        second = []
        for s in near:
            second.append(send(f"a_away{s}", view, view, device(q, s, h)))
        out += second
        for s in (2,):
            arrived(f"a_away{-s}", block)
            for t in (2, 1):
                v = amp.at[r, zpos(2)]
                out.append(send(f"a_on{t}", v, v, device(q, -t, h)))
            arrived(f"a_away{s}", block)
            v = amp.at[r, zpos(-2)]
            out.append(send("a_back", v, v, device(q, 1, h)))
        for s in (1, -1):
            arrived(f"a_away{s}", block)
        for step in (0, -2, 2, 1, -1, 4, -3, 3):
            arrived(f"cross{step}", block)
        for name, _ in late("a_", -1):
            arrived(name, block)
        for core in (0, 1):
            pltpu.make_async_remote_copy(
                src_ref=mate.at[mine_half], dst_ref=mate.at[mine_half], send_sem=mate_sems.at[2],
                recv_sem=mate_sems.at[core], device_id=other_core, device_id_type=MESH,
            ).wait_recv()
        for copy in out:
            copy.wait_send()

    full = jnp.concatenate([amp[0].reshape(VIRT, HALF), amp[1].reshape(VIRT, HALF)], axis=1).astype(F32)
    flip = full.T
    paired = (2.0 * full - flip).astype(BF)
    out_own[...] = jnp.dot(paired, mate[...], preferred_element_type=F32).astype(BF)
    turned = (2.0 * flip - full).astype(BF)
    out_mate[...] = jnp.dot(turned, own[...], preferred_element_type=F32).astype(BF)

    for copy in sent:
        copy.wait_send()
    mate_copy(h, g, mate_pair.at[g]).wait_send()

    @pl.when(q == h)
    def _():
        left("own_core", own)

    @pl.when(q != h)
    def _():
        for core in (0, 1):
            left(f"own_y{core}", own.at[mine_half])
        left("mate_core", mate_pair.at[h])


def on_device(blocks, vir_energy, occ_energy, partner):
    vir = vir_energy.astype(F32).reshape(6, 128)
    occ = jnp.broadcast_to(occ_energy.astype(F32).reshape(1, 1), (2, 128))
    energy = jnp.concatenate([vir, occ], axis=0)
    vmem = pl.BlockSpec(memory_space=pltpu.VMEM)
    unit = (BAND, HALF)
    gamma_own, gamma_mate = pl.pallas_call(
        kernel,
        out_shape=[jax.ShapeDtypeStruct((VIRT, COLS), BF)] * 2,
        in_specs=[pl.BlockSpec(memory_space=pltpu.SMEM), vmem, vmem],
        out_specs=[vmem, vmem],
        scratch_shapes=[
            pltpu.VMEM((NK, ROWS, COLS), BF),
            pltpu.VMEM((NK, ROWS, COLS), BF),
            pltpu.VMEM((2, VIRT, COLS), BF),
            pltpu.VMEM((2, HALF, COLS), BF),
            pltpu.VMEM((VIRT, COLS), BF),
            pltpu.VMEM((NK, 8, 128), F32),
            pltpu.VMEM((8, 128), F32),
            pltpu.VMEM((VIRT, 128), F32),
            pltpu.VMEM(unit, F32),
            pltpu.VMEM((8,) + unit, F32),
            pltpu.VMEM((5,) + unit, BF),
            pltpu.VMEM((3,) + unit, BF),
            pltpu.VMEM((2,) + unit, BF),
            pltpu.VMEM((2,) + unit, BF),
            pltpu.VMEM((2,) + unit, BF),
            pltpu.VMEM(unit, BF),
            pltpu.VMEM((2, 8) + unit, BF),
            DMA((N_MSG,)),
            DMA((N_MSG,)),
            DMA((3,)),
        ],
        compiler_params=pltpu.CompilerParams(
            collective_id=0, has_side_effects=True, vmem_limit_bytes=24 * 1024 * 1024
        ),
        name="pair_window",
    )(partner.reshape(NK), blocks[0], energy)
    return gamma_own[None], gamma_mate[None, None]


def solution(mesh):
    return jax.shard_map(
        on_device,
        mesh=mesh,
        in_specs=(P("kring", None, "cuts"), P("kring", None), P("kring"), P()),
        out_specs=(P("kring", None, "cuts"), P(None, "kring", None, "cuts")),
        check_vma=False,
    )
```

time: 378 us -> 61.1 us (0.16)
  the two profiles are of different devices: /device:TPU:2 before, /device:TPU:1 now
where the time goes in v2:
time: 61.1 us; the launch traced here: 61 us
  Pallas kernels  55.8 us (91%)
  local copies, waits for them, and re-layouts  3.8 us (6%)
  between operations  1.32 us (2%)
    pallas_call x1, Pallas kernels, on_device(): pl.pallas_call(kernel, out_shape=[jax.ShapeDtypeStruct((VIRT, COLS), BF)]...  55.8 us
    unnamed x8, local copies, waits for them, and re-layouts  3.8 us

profile of v2, /device:TPU:1, one launch (start us, length us, event | category | flops | bytes accessed | tf_op | source)
XLA Modules:
  0.0 61.0 jit_solution(5672536622682685828)
XLA Ops:
  1.3 0.0 copy-start.2
  1.3 0.7 %copy-done.2 = bf16[1,768]{1,0:T(2,128)(2,1)S(1)} copy-done((bf16[1,768]{1,0:T(2,128)(2,1)S(1)}, bf16[1,768]{1,0:T(2,128)(2,1)}, u32[]{:S(2)}) %copy-start.2) | copy-done | bytes 1560
  2.0 0.0 copy-start.1
  2.0 0.6 %copy-done.1 = s32[1,16]{1,0:T(1,128)S(1)} copy-done((s32[1,16]{1,0:T(1,128)S(1)}, s32[1,16]{1,0:T(1,128)}, u32[]{:S(2)}) %copy-start.1) | copy-done | bytes 88
  2.6 0.0 copy-start
  2.6 1.0 %copy-done = bf16[1,768,256]{2,1,0:T(8,128)(2,1)S(1)} copy-done((bf16[1,768,256]{2,1,0:T(8,128)(2,1)S(1)}, bf16[1,768,256]{2,1,0:T(8,128)(2,1)}, u32[]{:S(2)}) %copy-start) | copy-done | bytes 393240
  3.6 55.8 %pair_window.1 = (bf16[768,256]{1,0:T(8,128)(2,1)S(1)}, bf16[768,256]{1,0:T(8,128)(2,1)S(1)}) custom-call(s32[16]{0:T(128)S(1)} %bitcast.10, bf16[768,256]{1,0:T(8,128)(2,1)S(1)} %bitcast.7, f32[8,128]{1,0:T(8,128)S(1)} %pad_convert_fusion.energy), custom_call_target="tpu_custom_call" | custom-call | tf_op jit(solution)/shard_map/pair_window/pallas_call | solution.py:310
  59.5 0.7 %copy.9 = bf16[1,768,256]{2,1,0:T(8,128)(2,1)} copy(bf16[1,768,256]{2,1,0:T(8,128)(2,1)S(1)} %bitcast.9) | data formatting | bytes 786432
  60.2 0.7 %copy.10 = bf16[1,1,768,256]{3,2,1,0:T(8,128)(2,1)} copy(bf16[1,1,768,256]{3,2,1,0:T(8,128)(2,1)S(1)} %bitcast.8) | data formatting | bytes 786432
  (2 shorter events, 0.0 us)
Async XLA Ops:
  1.3 0.7 %copy-start.2 = (bf16[1,768]{1,0:T(2,128)(2,1)S(1)}, bf16[1,768]{1,0:T(2,128)(2,1)}, u32[]{:S(2)}) copy-start(bf16[1,768]{1,0:T(2,128)(2,1)} %param.5) | copy-start | bytes 4612
  2.0 0.7 %copy-start.1 = (s32[1,16]{1,0:T(1,128)S(1)}, s32[1,16]{1,0:T(1,128)}, u32[]{:S(2)}) copy-start(s32[1,16]{1,0:T(1,128)} %param.7) | copy-start | bytes 196
  2.6 1.0 %copy-start = (bf16[1,768,256]{2,1,0:T(8,128)(2,1)S(1)}, bf16[1,768,256]{2,1,0:T(8,128)(2,1)}, u32[]{:S(2)}) copy-start(bf16[1,768,256]{2,1,0:T(8,128)(2,1)} %param.4) | copy-start | bytes 1179652
